TPU v7x, 768 devices: a whole 4x8x12 slice. The times are simulated.
768 devices in a mesh: lat: 12 (over z_lo, core), lon: 16 (over z_hi, y), lev: 4 (over x).
Axes of the slice: x: 4, y: 8, z: 12 (z_hi: 2, z_lo: 6; z = z_hi * 6 + z_lo), core: 2. Of those that a mesh axis runs over, the one named last changes fastest.
Arguments:
- tokens: bfloat16 [4, 72, 384, 512], P('lev', 'lat', 'lon'), may hold values from -6 to 6
- norm_gain: float32 [2, 2, 512], replicated, may hold values from 0.25 to 1.75
- norm_offset: float32 [2, 2, 512], replicated, may hold values from -3 to 3
- w_qkv: bfloat16 [2, 512, 1536], replicated, may hold values from -0.25 to 0.25
- w_proj: bfloat16 [2, 512, 512], replicated, may hold values from -0.25 to 0.25
- w_up: bfloat16 [2, 512, 1024], replicated, may hold values from -0.25 to 0.25
- w_down: bfloat16 [2, 1024, 512], replicated, may hold values from -0.1875 to 0.1875
- rel_bias: float32 [2, 16, 37], replicated, may hold values from -4 to 720
Outputs:
- result: bfloat16 [4, 72, 384, 512], P('lev', 'lat', 'lon')
All inputs are finite; a program needn't handle non-finite values.
Results may differ from a plain program's by a relative error of at most 0.015.
Values may be sent and summed in bfloat16 or wider, within the bound.
No kernel may reach another device: no remote copies, remote signals or barrier semaphores. Data moves between devices by JAX's collectives and lax.ppermute only.
A program may use at most 64 MiB of HBM per device.

v0:
```python
import functools
import math

import jax
import jax.numpy as jnp
from jax import lax
from jax.experimental import pallas as pl
from jax.experimental.pallas import tpu as pltpu
from jax.sharding import PartitionSpec as P


D = 512
HEADS = 16
HEAD_DIM = 32
WLAT = 6
WLON = 12
WLEV = 2
EPS = 1e-05

QROWS, QCOLS = WLAT // 2, WLON // 2
QPAD = 48
HALF = 2 * QPAD
WROWS = 4 * QPAD
KEYS = 256
PLANE = WLAT * WLON
GROUP = 128 // HEAD_DIM
GROUPS = HEADS // GROUP
FEAT = WLAT + WLON + WLEV
FROWS = 24
NEG = -1e30
ROOT = math.sqrt(HEAD_DIM)
AXES = ("lat", "lon", "lev")


def f32dot(a, b):
    return jnp.dot(a, b, preferred_element_type=jnp.float32)


def layer_norm(values, gain, offset):
    average = jnp.mean(values, axis=-1, keepdims=True)
    centered = values - average
    variance = jnp.mean(centered * centered, axis=-1, keepdims=True)
    return centered * lax.rsqrt(variance + EPS) * gain + offset


def attend(query, bias_q, keys, values, key_feat):
    n = query.shape[0]
    lane_head = lax.broadcasted_iota(jnp.int32, (n, 128), 1) // HEAD_DIM
    pad = jnp.zeros((KEYS - WROWS, 128), jnp.bfloat16)
    ones = jnp.ones((KEYS, 128), jnp.bfloat16)
    outs = []
    for g in range(GROUPS):
        lanes = slice(g * 128, (g + 1) * 128)
        qg = query[:, lanes]
        lhs = jnp.concatenate(
            [
                jnp.concatenate(
                    [
                        jnp.where(lane_head == h, qg, jnp.zeros_like(qg)),
                        bias_q[:, (g * GROUP + h) * 128 : (g * GROUP + h + 1) * 128],
                    ],
                    axis=1,
                )
                for h in range(GROUP)
            ],
            axis=0,
        )
        rhs = jnp.concatenate(
            [jnp.concatenate([keys[:, lanes], pad], axis=0), key_feat], axis=1
        )
        scores = lax.dot_general(
            lhs, rhs, (((1,), (1,)), ((), ())), preferred_element_type=jnp.float32
        )
        top = jnp.max(scores, axis=-1, keepdims=True)
        weight = jnp.exp2((scores - top) * (math.log2(math.e) / ROOT)).astype(jnp.bfloat16)
        vals = jnp.concatenate(
            [jnp.concatenate([values[:, lanes], pad], axis=0), ones], axis=1
        )
        both = f32dot(weight, vals)
        total = both[:n]
        for h in range(1, GROUP):
            here = jnp.concatenate([lane_head, lane_head], axis=1) == h
            total = jnp.where(here, both[h * n : (h + 1) * n], total)
        outs.append((total[:, :128] / total[:, 128:]).astype(jnp.bfloat16))
    return jnp.concatenate(outs, axis=1)


def finish(tokens, mixture, gain, offset, w_proj, w_up, w_down):
    residual = (tokens + f32dot(mixture, w_proj)).astype(jnp.bfloat16).astype(jnp.float32)
    normed = layer_norm(residual, gain, offset).astype(jnp.bfloat16)
    hidden = jax.nn.gelu(f32dot(normed, w_up)).astype(jnp.bfloat16)
    return (residual + f32dot(hidden, w_down)).astype(jnp.bfloat16)


def place_of_device():
    i, j, l = (lax.axis_index(name) for name in AXES)
    wrap = (i == 0) | (i == lax.axis_size("lat") - 1)
    return l % 2, (l + j) % 2, i % 2, wrap


def steps(values, size, count):
    total = jnp.zeros_like(values)
    for k in range(1, count):
        total = total + (values >= k * size).astype(jnp.int32)
    return total


def column(rows):
    return lax.broadcasted_iota(jnp.int32, (rows, 1), 0)


def split_token(t):
    lv = steps(t, QROWS * QCOLS, 3)
    rest = t - lv * (QROWS * QCOLS)
    a = steps(rest, QCOLS, QROWS)
    return lv, a, rest - a * QCOLS


def split_window(w):
    a = steps(w, WLON, WLAT)
    return a, w - a * WLON


def onehot(index, columns):
    lane = lax.broadcasted_iota(jnp.int32, (index.shape[0], columns), 1)
    return (lane == index).astype(jnp.float32).astype(jnp.bfloat16)


def features(a, o, lv, real, width, copies, flags=()):
    lane = lax.broadcasted_iota(jnp.int32, (a.shape[0], width), 1)
    hit = jnp.zeros(lane.shape, jnp.float32)
    for k in range(copies):
        base = k * FEAT
        here = (lane == base + a) | (lane == base + WLAT + o) | (lane == base + WLAT + WLON + lv)
        hit = jnp.where(here, 1.0, hit)
    hit = jnp.where(real, hit, 0.0)
    for k, flag in enumerate(flags):
        hit = jnp.where((lane == copies * FEAT + k) & flag, 1.0, hit)
    return hit.astype(jnp.bfloat16)


def window_rows(side, odd, shifted):
    row = column(WROWS)
    quad = steps(row, QPAD, 4)
    sb = (quad >= 2).astype(jnp.int32)
    sa = quad - 2 * sb
    lv, a, o = split_token(row - quad * QPAD)
    low = jnp.where(sa == 0, 1 - odd, odd)
    east = jnp.where(sb == 0, 1 - side, side)
    if shifted:
        return lv, QROWS * (1 - low) + a, QCOLS * (1 - east) + o
    return lv, QROWS * low + a, QCOLS * east + o


def query_bias(b, spots, table, wrap, bias):
    lane = lax.broadcasted_iota(jnp.int32, (1, 256), 1) % 128
    masks = jnp.where(lane == 3 * FEAT, NEG, 0.0)
    if wrap is not None:
        masks = jnp.where((lane == 3 * FEAT + 1) & wrap, NEG, masks)
    for h in range(0, HEADS, 2):
        pair = [table[pl.ds(b * HEADS + h + k, FROWS, stride=2 * HEADS), :] for k in range(2)]
        rows = jnp.concatenate(pair, axis=1).astype(jnp.bfloat16)
        bias[:, h * 128 : (h + 2) * 128] = (f32dot(spots, rows) + masks).astype(jnp.bfloat16)


def cut_kernel(plane, out):
    _, side, _, _ = place_of_device()
    a, o = split_window(column(PLANE))
    source = a * (2 * WLON) + WLON * (1 - side) + o
    out[...] = f32dot(onehot(source, 2 * PLANE), plane[...]).astype(jnp.bfloat16)


def start_weights(b, sources, targets, sems):
    copies = [
        pltpu.make_async_copy(src.at[b], dst, sems.at[k])
        for k, (src, dst) in enumerate(zip(sources, targets, strict=True))
    ]
    for copy in copies:
        copy.start()
    return copies


def fill_table(rel_bias, table):
    scaled = rel_bias[...] * ROOT
    hi = scaled.astype(jnp.bfloat16)
    rest = scaled - hi.astype(jnp.float32)
    mid = rest.astype(jnp.bfloat16)
    low = (rest - mid.astype(jnp.float32)).astype(jnp.bfloat16)
    rows, count = rel_bias.shape
    n = lax.broadcasted_iota(jnp.int32, (1, FROWS * 128), 1)
    r, lane = n // 128, n % 128
    piece = steps(lane, FEAT, 4)
    c = lane - piece * FEAT
    lat = (r < WLAT) & (c < WLAT)
    lon = (r >= WLAT) & (c >= WLAT) & (r < WLAT + WLON) & (c < WLAT + WLON)
    lev = (r >= WLAT + WLON) & (r < FEAT) & (c >= WLAT + WLON)
    start = jnp.where(
        lat,
        WLAT - 1,
        jnp.where(lon, 2 * WLAT + WLON - 2, 2 * WLAT + 2 * WLON + WLEV - 3),
    )
    index = jnp.where(lat | lon | lev, start + r - c, -1)
    entry = lax.broadcasted_iota(jnp.int32, (count, FROWS * 128), 0)
    total = jnp.zeros((rows, FROWS * 128), jnp.float32)
    for k, part in enumerate((hi, mid, low)):
        hit = entry == jnp.where(piece == k, index, -1)
        total = total + f32dot(part, jnp.where(hit, 1.0, 0.0).astype(jnp.bfloat16))
    for r in range(FROWS):
        table[r * rows : (r + 1) * rows] = total[:, r * 128 : (r + 1) * 128]


def prepare_first(
    rel_bias, w_qkv, w_proj, w_up, w_down,
    pick, key_feat, bias, table, v_qkv, v_proj, v_up, v_down, sems,
):
    copies = start_weights(
        0, (w_qkv, w_proj, w_up, w_down), (v_qkv, v_proj, v_up, v_down), sems
    )
    fill_table(rel_bias, table)
    level, side, odd, _ = place_of_device()
    lv, a, o = window_rows(side, odd, False)
    mine = a * (2 * WLON) + WLON * side + o
    source = jnp.where(lv == level, mine, 2 * PLANE + a * WLON + o)
    source = jnp.where(lv < WLEV, source, -1)
    pick[...] = onehot(source, 3 * PLANE)
    real = lv < WLEV
    spots = features(a, o, lv, real, FROWS, 1)
    query_bias(0, spots, table, None, bias)
    key_feat[:WROWS] = features(a, o, lv, real, 128, 3, [~real])
    lane = lax.broadcasted_iota(jnp.int32, (KEYS - WROWS, 128), 1)
    key_feat[WROWS:] = jnp.where(lane == 3 * FEAT, 1.0, 0.0).astype(jnp.bfloat16)
    for copy in copies:
        copy.wait()


def prepare_second(
    after, table, w_qkv, w_proj, w_up, w_down,
    key_feat, bias, place, spread, v_qkv, v_proj, v_up, v_down, sems,
):
    del after
    copies = start_weights(
        1, (w_qkv, w_proj, w_up, w_down), (v_qkv, v_proj, v_up, v_down), sems
    )
    level, side, odd, wrap = place_of_device()
    lv, a, o = window_rows(side, odd, True)
    spots = features(a, o, lv, lv < WLEV, FROWS, 1)
    query_bias(1, spots, table, wrap, bias)
    row = column(KEYS)
    part = steps(row, QPAD, 5)
    lv, a, o = split_token(row - part * QPAD)
    real = (lv < WLEV) & (part < 4)
    across_lat = (part >= 2).astype(jnp.int32)
    across_lon = ((part == 1) | (part == 3)).astype(jnp.int32)
    for s_lon in range(2):
        for s_lat in range(2):
            own_low = odd if s_lat == 0 else 1 - odd
            own_east = side if s_lon == 0 else 1 - side
            low = jnp.where(across_lat == 1, 1 - own_low, own_low)
            east = jnp.where(across_lon == 1, 1 - own_east, own_east)
            flags = [~real] + ([real & (across_lat == 1)] if s_lat else [])
            key_feat[2 * s_lon + s_lat] = features(
                QROWS * low + a, QCOLS * east + o, lv, real, 128, 3, flags
            )
    row = column(2 * PLANE)
    other = (row >= PLANE).astype(jnp.int32)
    a, o = split_window(row - other * PLANE)
    at_level = jnp.where(other == 1, 1 - level, level)
    low, east = (a >= QROWS).astype(jnp.int32), (o >= QCOLS).astype(jnp.int32)
    sa = jnp.where(low == 1 - odd, 0, 1)
    sb = jnp.where(east == 1 - side, 0, 1)
    target = (2 * sb + sa) * QPAD + at_level * (QROWS * QCOLS)
    place[...] = onehot(target + (a - QROWS * low) * QCOLS + o - QCOLS * east, WROWS)
    a = steps(row, 2 * WLON, WLAT)
    c = row - a * (2 * WLON)
    right = (c >= WLON).astype(jnp.int32)
    at = a * WLON + c - WLON * right
    spread[...] = onehot(jnp.where(right == side, at, PLANE + at), 2 * PLANE)
    for copy in copies:
        copy.wait()


def first_kernel(
    own, other, pick, bias, key_feat, gain, offset, w_qkv, w_proj, w_up, w_down, out, near, far
):
    gain, offset = gain.at[0], offset.at[0]
    tokens = f32dot(pick[:, : 2 * PLANE], own[...]) + f32dot(pick[:, 2 * PLANE :], other[...])
    normed = layer_norm(tokens, gain[0:1], offset[0:1]).astype(jnp.bfloat16)
    packed = f32dot(normed, w_qkv[...]).astype(jnp.bfloat16)
    mixture = attend(
        packed[:, :D], bias, packed[:, D : 2 * D], packed[:, 2 * D :], key_feat[...]
    )
    result = finish(
        tokens, mixture, gain[1:2], offset[1:2], w_proj[...], w_up[...], w_down[...]
    )
    out[...] = result
    near[...] = result[:HALF]
    far[...] = result[HALF:]


def strip_kernel(own, lon, lat_a, lat_b):
    for k, out in enumerate((lat_a, lat_b)):
        for at, (ref, quad) in enumerate(((own, k), (own, 2 + k), (lon, k))):
            out[at * QPAD : (at + 1) * QPAD] = ref[quad * QPAD : (quad + 1) * QPAD]


def corner_kernel(own, lon, lat_a, lat_b):
    _, _, _, wrap = place_of_device()
    lat_a[...] = lon[:QPAD]

    @pl.when(wrap)
    def _():
        lat_b[...] = own[3 * QPAD :]

    @pl.when(jnp.logical_not(wrap))
    def _():
        lat_b[...] = lon[QPAD:]


def near_kernel(
    own, lon, lat_a, lat_b, bias, key_feat,
    gain, offset, w_qkv, w_proj, w_up, w_down, done, query_far, kv_far, kv,
):
    gain, offset = gain.at[1], offset.at[1]
    g0, o0 = gain[0:1], offset[0:1]
    tokens = own[...].astype(jnp.float32)
    normed = layer_norm(tokens, g0, o0).astype(jnp.bfloat16)
    query = f32dot(normed, w_qkv[:, :D]).astype(jnp.bfloat16)
    kv[:WROWS] = f32dot(normed, w_qkv[:, D:]).astype(jnp.bfloat16)
    base = WROWS
    for ref in (lon, lat_a, lat_b):
        more = layer_norm(ref[...].astype(jnp.float32), g0, o0).astype(jnp.bfloat16)
        kv[base : base + ref.shape[0]] = f32dot(more, w_qkv[:, D:]).astype(jnp.bfloat16)
        base += ref.shape[0]
    parts = []
    for sa in range(2):
        lat = WROWS + HALF + sa * 3 * QPAD
        rows = (sa * QPAD, WROWS + sa * QPAD, lat, lat + 2 * QPAD)
        window = jnp.concatenate([kv[r : r + QPAD] for r in rows], axis=0)
        q = slice(sa * QPAD, (sa + 1) * QPAD)
        parts.append(attend(query[q], bias.at[q], window[:, :D], window[:, D:], key_feat[sa]))
        kv_far[2 * sa * QPAD : (2 * sa + 1) * QPAD] = kv[HALF + sa * QPAD : HALF + (sa + 1) * QPAD]
        kv_far[(2 * sa + 1) * QPAD : (2 * sa + 2) * QPAD] = kv[lat + QPAD : lat + 2 * QPAD]
    query_far[...] = query[HALF:]
    done[...] = finish(
        tokens[:HALF], jnp.concatenate(parts, axis=0), gain[1:2], offset[1:2],
        w_proj[...], w_up[...], w_down[...],
    )


def far_kernel(
    own, done, query, kv_near, lon, lat_a, lat_b, bias, key_feat, place,
    gain, offset, w_qkv, w_proj, w_up, w_down, keep, send,
):
    gain, offset = gain.at[1], offset.at[1]
    late = jnp.concatenate([lon[...], lat_a[...], lat_b[...]], axis=0).astype(jnp.float32)
    normed = layer_norm(late, gain[0:1], offset[0:1]).astype(jnp.bfloat16)
    kv = f32dot(normed, w_qkv[:, D:]).astype(jnp.bfloat16)
    parts = []
    for sa in range(2):
        near = 2 * sa * QPAD
        window = jnp.concatenate(
            [
                kv_near[near : near + QPAD],
                kv[sa * QPAD : (sa + 1) * QPAD],
                kv_near[near + QPAD : near + 2 * QPAD],
                kv[(2 + sa) * QPAD : (3 + sa) * QPAD],
            ],
            axis=0,
        )
        q = slice(sa * QPAD, (sa + 1) * QPAD)
        b = slice(HALF + sa * QPAD, HALF + (sa + 1) * QPAD)
        parts.append(attend(query[q], bias.at[b], window[:, :D], window[:, D:], key_feat[2 + sa]))
    result = finish(
        own[HALF:].astype(jnp.float32), jnp.concatenate(parts, axis=0), gain[1:2], offset[1:2],
        w_proj[...], w_up[...], w_down[...],
    )
    both = f32dot(place[:, :HALF], done[...]) + f32dot(place[:, HALF:], result)
    keep[...] = both[:PLANE].astype(jnp.bfloat16)
    send[...] = both[PLANE:].astype(jnp.bfloat16)


def merge_kernel(mine, theirs, spread, out):
    both = f32dot(spread[:, :PLANE], mine[...]) + f32dot(spread[:, PLANE:], theirs[...])
    out[...] = both.astype(jnp.bfloat16)


def call(kernel, outs, args, scratch=(), flops=0, skip=(), wide=(), vmem=24 << 20):
    specs = [
        pl.BlockSpec(memory_space=pltpu.HBM if k in skip else pltpu.VMEM) for k in range(len(args))
    ]
    return pl.pallas_call(
        kernel,
        out_shape=[
            jax.ShapeDtypeStruct(s, jnp.float32 if k in wide else jnp.bfloat16)
            for k, s in enumerate(outs)
        ],
        in_specs=specs,
        out_specs=[pl.BlockSpec(memory_space=pltpu.VMEM)] * len(outs),
        scratch_shapes=list(scratch),
        compiler_params=pltpu.CompilerParams(vmem_limit_bytes=vmem),
        cost_estimate=pl.CostEstimate(flops=flops, bytes_accessed=1 << 20, transcendentals=0),
    )(*args)


def routes(mesh_shape):
    n_lat, n_lon, n_lev = mesh_shape

    def pairs(move):
        flat = lambda i, j, l: ((i % n_lat) * n_lon + j % n_lon) * n_lev + l
        return [
            (flat(i, j, l), flat(*move(i, j, l)))
            for i in range(n_lat)
            for j in range(n_lon)
            for l in range(n_lev)
        ]

    lat_b = lambda i: i + 1 if i % 2 else i - 1
    lon_b = lambda j, l: j + 1 if (l + j) % 2 else j - 1
    ends = (0, n_lat - 1)
    return {
        "lev": pairs(lambda i, j, l: (i, j, l ^ 1)),
        "lon": pairs(lambda i, j, l: (i, lon_b(j, l), l)),
        "lat_a": pairs(lambda i, j, l: (i ^ 1, j, l)),
        "lat_b": pairs(lambda i, j, l: (lat_b(i), j, l)),
        "corner": pairs(lambda i, j, l: (lat_b(i), lon_b(j, l) if i in ends else j, l)),
    }


def shards(mesh_shape, tokens, norm_gain, norm_offset, w_qkv, w_proj, w_up, w_down, rel_bias):
    send_to = routes(mesh_shape)
    swap = lambda x, name: lax.ppermute(x, AXES, send_to[name])
    norms = (norm_gain, norm_offset)
    raw = tuple(
        pltpu.with_memory_space_constraint(w, pltpu.HBM) for w in (w_qkv, w_proj, w_up, w_down)
    )
    shapes = [w.shape[1:] for w in raw]
    sems = [pltpu.SemaphoreType.DMA((len(raw),))]

    plane = tokens.reshape(2 * PLANE, D)
    (cut,) = call(cut_kernel, [(PLANE, D)], (plane,), flops=10**7)
    other = swap(cut, "lev")
    pick, feat_first, bias_first, table, *weights = call(
        prepare_first,
        [(WROWS, 3 * PLANE), (KEYS, 128), (WROWS, HEADS * 128), (FROWS * 2 * HEADS, 128)] + shapes,
        (rel_bias.reshape(2 * HEADS, rel_bias.shape[-1]),) + raw,
        scratch=sems,
        flops=10**8,
        skip=(1, 2, 3, 4),
        wide=(3,),
    )
    first, near, far = call(
        first_kernel,
        [(WROWS, D), (HALF, D), (HALF, D)],
        (plane, other, pick, bias_first, feat_first) + norms + tuple(weights),
        flops=2 * 10**9,
    )

    lon_b = swap(far, "lon")
    lon_a = swap(near, "lev")
    feat_second, bias_second, place, spread, *weights = call(
        prepare_second,
        [(4, KEYS, 128), (WROWS, HEADS * 128), (2 * PLANE, WROWS), (2 * PLANE, 2 * PLANE)] + shapes,
        (first, table) + raw,
        scratch=sems,
        flops=10**8,
        skip=(2, 3, 4, 5),
    )
    weights = norms + tuple(weights)
    strip_a, strip_b = call(strip_kernel, [(3 * QPAD, D)] * 2, (first, lon_a), flops=10**6)
    lat_b = swap(strip_b, "lat_b")
    lat_a = swap(strip_a, "lat_a")
    done, query_far, kv_far = call(
        near_kernel,
        [(HALF, D), (HALF, D), (WROWS, 2 * D)],
        (first, lon_a, lat_a, lat_b, bias_second, feat_second) + weights,
        scratch=[pltpu.VMEM((WROWS + HALF + 6 * QPAD, 2 * D), jnp.bfloat16)],
        flops=2 * 10**9,
    )

    corner_a, corner_b = call(corner_kernel, [(QPAD, D)] * 2, (first, lon_b), flops=10**6)
    corner_b = swap(corner_b, "corner")
    corner_a = swap(corner_a, "lat_a")
    keep, send = call(
        far_kernel,
        [(PLANE, D), (PLANE, D)],
        (first, done, query_far, kv_far, lon_b, corner_a, corner_b, bias_second, feat_second, place)
        + weights,
        flops=2 * 10**9,
    )
    theirs = swap(send, "lev")
    (result,) = call(merge_kernel, [(2 * PLANE, D)], (keep, theirs, spread), flops=10**8)
    return result.reshape(1, WLAT, 2 * WLON, D)


def solution(mesh):
    shape = tuple(mesh.shape[name] for name in AXES)
    return jax.shard_map(
        functools.partial(shards, shape),
        mesh=mesh,
        in_specs=(P("lev", "lat", "lon", None), P(), P(), P(), P(), P(), P(), P()),
        out_specs=P("lev", "lat", "lon", None),
        check_vma=False,
    )
```

profile of v0, /device:TPU:4, one launch (start us, length us, event | category | flops | bytes accessed | tf_op | source)
XLA Modules:
  0.0 71.8 jit_solution(14762679756764683706)
XLA Ops:
  0.0 0.0 copy-start
  0.0 0.9 %copy-done = bf16[1,6,24,512]{3,2,1,0:T(8,128)(2,1)S(1)} copy-done((bf16[1,6,24,512]{3,2,1,0:T(8,128)(2,1)S(1)}, bf16[1,6,24,512]{3,2,1,0:T(8,128)(2,1)}, u32[]{:S(2)}) %copy-start) | copy-done | bytes 147480
  0.9 0.2 shard_map.82
  1.1 3.1 %collective-permute-start = (bf16[72,512]{1,0:T(8,128)(2,1)S(1)}, bf16[72,512]{1,0:T(8,128)(2,1)S(1)}, u32[]{:S(2)}, u32[]{:S(2)}) collective-permute-start(bf16[72,512]{1,0:T(8,128)(2,1)S(1)} %shard_map.82), channel_id=1, source_target_pairs={{0,1},{1,0},{2,3},{3,2},{4,5},{5,4},{6,7},{7,6},{8,9},{9,8},{10,11... | collective-permute-start | bytes 221192 | tf_op jit(solution)/shard_map/ppermute | solution.py:431
  4.2 0.0 copy-start.2
  4.2 0.7 copy-done.2
  4.9 0.0 copy-start.1
  4.9 0.0 copy-start.3
  4.9 0.0 copy-start.4
  4.9 2.5 %shard_map.83 = (bf16[192,216]{1,0:T(8,128)(2,1)S(1)}, bf16[256,128]{1,0:T(8,128)(2,1)S(1)}, bf16[192,2048]{1,0:T(8,128)(2,1)S(1)}, f32[768,128]{1,0:T(8,128)S(1...) custom-call(f32[32,37]{1,0:T(8,128)S(1)} %bitcast.5, ...), custom_call_target="tpu_custom_call" | custom-call | flops 100000000 | bytes 1048576 | tf_op jit(solution)/shard_map/pallas_call | solution.py:391
  7.4 0.0 collective-permute-done.other
  7.4 0.0 copy-done.1
  7.4 0.0 copy-done.3
  7.4 0.0 copy-done.4
  7.5 3.2 %shard_map.84 = (bf16[192,512]{1,0:T(8,128)(2,1)S(1)}, bf16[96,512]{1,0:T(8,128)(2,1)S(1)}, bf16[96,512]{1,0:T(8,128)(2,1)S(1)}) custom-call(bf16[144,512]{1,0:T(8,128)(2,1)S(1)} %bitcast.4, bf16[72,512]{1,0:T(8,128)(2,1)S(1)} %collective-permute-done.other, bf16[192,216]{1,0:T(8,128)(2,1)S(1)} %get-tuple-element.33.pick, ...), custom_call_target="tpu_custom_call" | custom-call | flops 2000000000 | bytes 1048576 | tf_op jit(solution)/shard_map/pallas_call | solution.py:391
  10.6 3.0 %collective-permute-start.1 = (bf16[96,512]{1,0:T(8,128)(2,1)S(1)}, bf16[96,512]{1,0:T(8,128)(2,1)S(1)}, u32[]{:S(2)}, u32[]{:S(2)}) collective-permute-start(bf16[96,512]{1,0:T(8,128)(2,1)S(1)} %get-tuple-element.41), channel_id=1, source_target_pairs={{0,1},{1,0},{2,3},{3,2},{4,5},{5,4},{6,7},{7,6},{8,9},{9,8},{10,11... | collective-permute-start | bytes 294920 | tf_op jit(solution)/shard_map/ppermute | solution.py:431
  13.6 3.5 %collective-permute-done.1.lon = bf16[96,512]{1,0:T(8,128)(2,1)S(1)} collective-permute-done((bf16[96,512]{1,0:T(8,128)(2,1)S(1)}, bf16[96,512]{1,0:T(8,128)(2,1)S(1)}, u32[]{:S(2)}, u32[]{:S(2)}) %collective-permute-start.1) | collective-permute-done | bytes 98336 | tf_op jit(solution)/shard_map/ppermute | solution.py:431
  17.2 1.9 %collective-permute-start.2 = (bf16[144,512]{1,0:T(8,128)(2,1)S(1)}, bf16[144,512]{1,0:T(8,128)(2,1)S(1)}, u32[]{:S(2)}, u32[]{:S(2)}) collective-permute-start(bf16[144,512]{1,0:T(8,128)(2,1)S(1)} %get-tuple-element.42), channel_id=1, source_target_pairs={{0,64},{1,65},{2,66},{3,67},{4,68},{5,69},{6,70},{7,71},{8,72},{9,... | collective-permute-start | bytes 442376 | tf_op jit(solution)/shard_map/ppermute | solution.py:431
  19.1 12.8 %collective-permute-start.3 = (bf16[144,512]{1,0:T(8,128)(2,1)S(1)}, bf16[144,512]{1,0:T(8,128)(2,1)S(1)}, u32[]{:S(2)}, u32[]{:S(2)}) collective-permute-start(bf16[144,512]{1,0:T(8,128)(2,1)S(1)} %get-tuple-element.43), channel_id=1, source_target_pairs={{0,704},{1,705},{2,706},{3,707},{4,708},{5,709},{6,710},{7,711},{8... | collective-permute-start | bytes 442376 | tf_op jit(solution)/shard_map/ppermute | solution.py:431
  31.9 13.0 %collective-permute-start.4 = (bf16[96,512]{1,0:T(8,128)(2,1)S(1)}, bf16[96,512]{1,0:T(8,128)(2,1)S(1)}, u32[]{:S(2)}, u32[]{:S(2)}) collective-permute-start(bf16[96,512]{1,0:T(8,128)(2,1)S(1)} %get-tuple-element.54), channel_id=1, source_target_pairs={{0,60},{1,5},{2,62},{3,7},{4,8},{5,1},{6,10},{7,3},{8,4},{9,13},{1... | collective-permute-start | bytes 294920 | tf_op jit(solution)/shard_map/ppermute | solution.py:431
  44.9 2.3 %shard_map.86 = (bf16[4,256,128]{2,1,0:T(8,128)(2,1)S(1)}, bf16[192,2048]{1,0:T(8,128)(2,1)S(1)}, bf16[144,192]{1,0:T(8,128)(2,1)S(1)}, bf16[144,144]{1,0:T(8,12...) custom-call(bf16[192,512]{1,0:T(8,128)(2,1)S(1)} %get-tuple-element., ...), custom_call_target="tpu_custom_call" | custom-call | flops 100000000 | bytes 1048576 | tf_op jit(solution)/shard_map/pallas_call | solution.py:391
  47.2 0.3 collective-permute-done.4.lon
  47.5 1.9 %collective-permute-start.5 = (bf16[48,512]{1,0:T(8,128)(2,1)S(1)}, bf16[48,512]{1,0:T(8,128)(2,1)S(1)}, u32[]{:S(2)}, u32[]{:S(2)}) collective-permute-start(bf16[48,512]{1,0:T(8,128)(2,1)S(1)} %get-tuple-element.55), channel_id=1, source_target_pairs={{0,64},{1,65},{2,66},{3,67},{4,68},{5,69},{6,70},{7,71},{8,72},{9,... | collective-permute-start | bytes 147464 | tf_op jit(solution)/shard_map/ppermute | solution.py:431
  49.4 7.5 %collective-permute-start.6 = (bf16[48,512]{1,0:T(8,128)(2,1)S(1)}, bf16[48,512]{1,0:T(8,128)(2,1)S(1)}, u32[]{:S(2)}, u32[]{:S(2)}) collective-permute-start(bf16[48,512]{1,0:T(8,128)(2,1)S(1)} %get-tuple-element.56), channel_id=1, source_target_pairs={{0,764},{1,709},{2,766},{3,711},{4,712},{5,705},{6,714},{7,707},{8... | collective-permute-start | bytes 147464 | tf_op jit(solution)/shard_map/ppermute | solution.py:431
  56.9 0.0 collective-permute-done.2.lat_a
  56.9 0.0 collective-permute-done.3.lat_b
  56.9 3.9 %shard_map.87 = (bf16[96,512]{1,0:T(8,128)(2,1)S(1)}, bf16[96,512]{1,0:T(8,128)(2,1)S(1)}, bf16[192,1024]{1,0:T(8,128)(2,1)S(1)}) custom-call(bf16[192,512]{1,0:T(8,128)(2,1)S(1)} %get-tuple-element.40.own.after, bf16[96,512]{1,0:T(8,128)(2,1)S(1)} %collective-permute-done.1.lon, bf16[144,512]{1,0:T(8,128)(2,1)S(1)} %collective-permute-done.2.lat_a, ...), custom_call_target="tpu_custom_call" | custom-call | flops 2000000000 | bytes 1048576 | tf_op jit(solution)/shard_map/pallas_call | solution.py:391
  60.9 0.0 collective-permute-done.5.lat_a
  60.9 0.0 collective-permute-done.6.lat_b
  60.9 3.7 %shard_map.89 = (bf16[72,512]{1,0:T(8,128)(2,1)S(1)}, bf16[72,512]{1,0:T(8,128)(2,1)S(1)}) custom-call(bf16[192,512]{1,0:T(8,128)(2,1)S(1)} %get-tuple-element.40.own.after, bf16[96,512]{1,0:T(8,128)(2,1)S(1)} %get-tuple-element.51.done, bf16[96,512]{1,0:T(8,128)(2,1)S(1)} %get-tuple-element.52.query, bf16[192,1024]{1,0:T(8,128)(2,1)S(1)} %get-tuple-element.53.kv_near, ...), custom_call_target="tpu_custom_call" | custom-call | flops 2000000000 | bytes 1048576 | tf_op jit(solution)/shard_map/pallas_call | solution.py:391
  64.6 1.9 %collective-permute-start.7 = (bf16[72,512]{1,0:T(8,128)(2,1)S(1)}, bf16[72,512]{1,0:T(8,128)(2,1)S(1)}, u32[]{:S(2)}, u32[]{:S(2)}) collective-permute-start(bf16[72,512]{1,0:T(8,128)(2,1)S(1)} %get-tuple-element.59), channel_id=1, source_target_pairs={{0,1},{1,0},{2,3},{3,2},{4,5},{5,4},{6,7},{7,6},{8,9},{9,8},{10,11... | collective-permute-start | bytes 221192 | tf_op jit(solution)/shard_map/ppermute | solution.py:431
  66.5 4.3 %collective-permute-done.7.theirs = bf16[72,512]{1,0:T(8,128)(2,1)S(1)} collective-permute-done((bf16[72,512]{1,0:T(8,128)(2,1)S(1)}, bf16[72,512]{1,0:T(8,128)(2,1)S(1)}, u32[]{:S(2)}, u32[]{:S(2)}) %collective-permute-start.7) | collective-permute-done | bytes 73760 | tf_op jit(solution)/shard_map/ppermute | solution.py:431
  70.9 0.9 %shard_map.90 = bf16[144,512]{1,0:T(8,128)(2,1)} custom-call(bf16[72,512]{1,0:T(8,128)(2,1)S(1)} %get-tuple-element.58.mine, bf16[72,512]{1,0:T(8,128)(2,1)S(1)} %collective-permute-done.7.theirs, bf16[144,144]{1,0:T(8,128)(2,1)S(1)} %get-tuple-element.60.spread), custom_call_target="tpu_custom_call" | custom-call | flops 100000000 | bytes 1048576 | tf_op jit(solution)/shard_map/pallas_call | solution.py:391
  (2 shorter events, 0.0 us)
Async XLA Ops:
  0.0 0.9 %copy-start = (bf16[1,6,24,512]{3,2,1,0:T(8,128)(2,1)S(1)}, bf16[1,6,24,512]{3,2,1,0:T(8,128)(2,1)}, u32[]{:S(2)}) copy-start(bf16[1,6,24,512]{3,2,1,0:T(8,128)(2,1)} %param.8) | copy-start | bytes 442372
  1.1 6.4 %collective-permute-start = (bf16[72,512]{1,0:T(8,128)(2,1)S(1)}, bf16[72,512]{1,0:T(8,128)(2,1)S(1)}, u32[]{:S(2)}, u32[]{:S(2)}) collective-permute-start(bf16[72,512]{1,0:T(8,128)(2,1)S(1)} %shard_map.82), channel_id=1, source_target_pairs={{0,1},{1,0},{2,3},{3,2},{4,5},{5,4},{6,7},{7,6},{8,9},{9,8},{10,11... | collective-permute-start | bytes 221192 | tf_op jit(solution)/shard_map/ppermute | solution.py:431
  4.2 0.7 %copy-start.2 = (f32[2,16,37]{2,1,0:T(8,128)S(1)}, f32[2,16,37]{2,1,0:T(8,128)}, u32[]{:S(2)}) copy-start(f32[2,16,37]{2,1,0:T(8,128)} %param.15) | copy-start | bytes 14212
  4.9 2.5 %copy-start.1 = (bf16[1,6,24,512]{3,2,1,0:T(8,128)(2,1)S(1)}, bf16[1,6,24,512]{3,2,1,0:T(8,128)(2,1)}, u32[]{:S(2)}) copy-start(bf16[1,6,24,512]{3,2,1,0:T(8,128)(2,1)} %param.8) | copy-start | bytes 442372
  4.9 2.5 %copy-start.3 = (f32[2,2,512]{2,1,0:T(2,128)S(1)}, f32[2,2,512]{2,1,0:T(2,128)}, u32[]{:S(2)}) copy-start(f32[2,2,512]{2,1,0:T(2,128)} %gain.5) | copy-start | bytes 24580
  4.9 2.5 %copy-start.4 = (f32[2,2,512]{2,1,0:T(2,128)S(1)}, f32[2,2,512]{2,1,0:T(2,128)}, u32[]{:S(2)}) copy-start(f32[2,2,512]{2,1,0:T(2,128)} %offset.5) | copy-start | bytes 24580
  10.6 6.5 %collective-permute-start.1 = (bf16[96,512]{1,0:T(8,128)(2,1)S(1)}, bf16[96,512]{1,0:T(8,128)(2,1)S(1)}, u32[]{:S(2)}, u32[]{:S(2)}) collective-permute-start(bf16[96,512]{1,0:T(8,128)(2,1)S(1)} %get-tuple-element.41), channel_id=1, source_target_pairs={{0,1},{1,0},{2,3},{3,2},{4,5},{5,4},{6,7},{7,6},{8,9},{9,8},{10,11... | collective-permute-start | bytes 294920 | tf_op jit(solution)/shard_map/ppermute | solution.py:431
  17.2 39.7 %collective-permute-start.2 = (bf16[144,512]{1,0:T(8,128)(2,1)S(1)}, bf16[144,512]{1,0:T(8,128)(2,1)S(1)}, u32[]{:S(2)}, u32[]{:S(2)}) collective-permute-start(bf16[144,512]{1,0:T(8,128)(2,1)S(1)} %get-tuple-element.42), channel_id=1, source_target_pairs={{0,64},{1,65},{2,66},{3,67},{4,68},{5,69},{6,70},{7,71},{8,72},{9,... | collective-permute-start | bytes 442376 | tf_op jit(solution)/shard_map/ppermute | solution.py:431
  19.1 37.8 %collective-permute-start.3 = (bf16[144,512]{1,0:T(8,128)(2,1)S(1)}, bf16[144,512]{1,0:T(8,128)(2,1)S(1)}, u32[]{:S(2)}, u32[]{:S(2)}) collective-permute-start(bf16[144,512]{1,0:T(8,128)(2,1)S(1)} %get-tuple-element.43), channel_id=1, source_target_pairs={{0,704},{1,705},{2,706},{3,707},{4,708},{5,709},{6,710},{7,711},{8... | collective-permute-start | bytes 442376 | tf_op jit(solution)/shard_map/ppermute | solution.py:431
  31.9 15.5 %collective-permute-start.4 = (bf16[96,512]{1,0:T(8,128)(2,1)S(1)}, bf16[96,512]{1,0:T(8,128)(2,1)S(1)}, u32[]{:S(2)}, u32[]{:S(2)}) collective-permute-start(bf16[96,512]{1,0:T(8,128)(2,1)S(1)} %get-tuple-element.54), channel_id=1, source_target_pairs={{0,60},{1,5},{2,62},{3,7},{4,8},{5,1},{6,10},{7,3},{8,4},{9,13},{1... | collective-permute-start | bytes 294920 | tf_op jit(solution)/shard_map/ppermute | solution.py:431
  47.5 13.4 %collective-permute-start.5 = (bf16[48,512]{1,0:T(8,128)(2,1)S(1)}, bf16[48,512]{1,0:T(8,128)(2,1)S(1)}, u32[]{:S(2)}, u32[]{:S(2)}) collective-permute-start(bf16[48,512]{1,0:T(8,128)(2,1)S(1)} %get-tuple-element.55), channel_id=1, source_target_pairs={{0,64},{1,65},{2,66},{3,67},{4,68},{5,69},{6,70},{7,71},{8,72},{9,... | collective-permute-start | bytes 147464 | tf_op jit(solution)/shard_map/ppermute | solution.py:431
  49.4 11.5 %collective-permute-start.6 = (bf16[48,512]{1,0:T(8,128)(2,1)S(1)}, bf16[48,512]{1,0:T(8,128)(2,1)S(1)}, u32[]{:S(2)}, u32[]{:S(2)}) collective-permute-start(bf16[48,512]{1,0:T(8,128)(2,1)S(1)} %get-tuple-element.56), channel_id=1, source_target_pairs={{0,764},{1,709},{2,766},{3,711},{4,712},{5,705},{6,714},{7,707},{8... | collective-permute-start | bytes 147464 | tf_op jit(solution)/shard_map/ppermute | solution.py:431
  64.6 6.2 %collective-permute-start.7 = (bf16[72,512]{1,0:T(8,128)(2,1)S(1)}, bf16[72,512]{1,0:T(8,128)(2,1)S(1)}, u32[]{:S(2)}, u32[]{:S(2)}) collective-permute-start(bf16[72,512]{1,0:T(8,128)(2,1)S(1)} %get-tuple-element.59), channel_id=1, source_target_pairs={{0,1},{1,0},{2,3},{3,2},{4,5},{5,4},{6,7},{7,6},{8,9},{9,8},{10,11... | collective-permute-start | bytes 221192 | tf_op jit(solution)/shard_map/ppermute | solution.py:431
where the time goes:
time: 72.2 us; the launch traced here: 71.8 us
  starting transfers between devices  45.1 us (62%)
  Pallas kernels  16.8 us (23%)
  waiting for transfers between devices  8.12 us (11%)
  local copies, waits for them, and re-layouts  1.63 us (2%)
    ppermute x8, starting transfers between devices, shards(): swap = lambda x, name: lax.ppermute(x, AXES, send_to[name])  45.1 us
    pallas_call x9, Pallas kernels, call(): pl.pallas_call(kernel, out_shape=[jax.ShapeDtypeStruct(s, jnp.float32 if...  16.8 us
    ppermute x8, waiting for transfers between devices, shards(): swap = lambda x, name: lax.ppermute(x, AXES, send_to[name])  8.12 us
    unnamed x10, local copies, waits for them, and re-layouts  1.63 us
  transfers between devices with their start and end apart: 8, of which 3 were waited for; matrix products, arithmetic and copies ran while one was open for 0% of the time, Pallas kernels for 12%

commit v1 on v0

--- a/solution.py
+++ b/solution.py
@@ -180,43 +180,43 @@
     return copies
 
 
-def fill_table(rel_bias, table):
-    scaled = rel_bias[...] * ROOT
+def fill_table(scaled, table):
     hi = scaled.astype(jnp.bfloat16)
     rest = scaled - hi.astype(jnp.float32)
     mid = rest.astype(jnp.bfloat16)
     low = (rest - mid.astype(jnp.float32)).astype(jnp.bfloat16)
-    rows, count = rel_bias.shape
-    n = lax.broadcasted_iota(jnp.int32, (1, FROWS * 128), 1)
-    r, lane = n // 128, n % 128
-    piece = steps(lane, FEAT, 4)
-    c = lane - piece * FEAT
+    rows, count = scaled.shape
+    width = FROWS * 128
+    n = lax.broadcasted_iota(jnp.int32, (1, width), 1)
+    r, c = n // 128, n % 128
     lat = (r < WLAT) & (c < WLAT)
     lon = (r >= WLAT) & (c >= WLAT) & (r < WLAT + WLON) & (c < WLAT + WLON)
-    lev = (r >= WLAT + WLON) & (r < FEAT) & (c >= WLAT + WLON)
+    lev = (r >= WLAT + WLON) & (r < FEAT) & (c >= WLAT + WLON) & (c < FEAT)
     start = jnp.where(
         lat,
         WLAT - 1,
         jnp.where(lon, 2 * WLAT + WLON - 2, 2 * WLAT + 2 * WLON + WLEV - 3),
     )
     index = jnp.where(lat | lon | lev, start + r - c, -1)
-    entry = lax.broadcasted_iota(jnp.int32, (count, FROWS * 128), 0)
-    total = jnp.zeros((rows, FROWS * 128), jnp.float32)
-    for k, part in enumerate((hi, mid, low)):
-        hit = entry == jnp.where(piece == k, index, -1)
-        total = total + f32dot(part, jnp.where(hit, 1.0, 0.0).astype(jnp.bfloat16))
+    entry = lax.broadcasted_iota(jnp.int32, (count, width), 0)
+    hit = jnp.where(entry == index, 1.0, 0.0).astype(jnp.bfloat16)
+    found = f32dot(jnp.concatenate([hi, mid, low], axis=0), hit)
+    total = found[:rows]
+    for k in (1, 2):
+        total = total + pltpu.roll(found[k * rows : (k + 1) * rows], k * FEAT, 1)
     for r in range(FROWS):
         table[r * rows : (r + 1) * rows] = total[:, r * 128 : (r + 1) * 128]
 
 
 def prepare_first(
     rel_bias, w_qkv, w_proj, w_up, w_down,
-    pick, key_feat, bias, table, v_qkv, v_proj, v_up, v_down, sems,
+    pick, key_feat, bias, table, v_qkv, v_proj, v_up, v_down, entries, sems,
 ):
+    fetch = pltpu.make_async_copy(rel_bias, entries, sems.at[4])
+    fetch.start()
     copies = start_weights(
         0, (w_qkv, w_proj, w_up, w_down), (v_qkv, v_proj, v_up, v_down), sems
     )
-    fill_table(rel_bias, table)
     level, side, odd, _ = place_of_device()
     lv, a, o = window_rows(side, odd, False)
     mine = a * (2 * WLON) + WLON * side + o
@@ -225,19 +225,20 @@
     pick[...] = onehot(source, 3 * PLANE)
     real = lv < WLEV
     spots = features(a, o, lv, real, FROWS, 1)
-    query_bias(0, spots, table, None, bias)
     key_feat[:WROWS] = features(a, o, lv, real, 128, 3, [~real])
     lane = lax.broadcasted_iota(jnp.int32, (KEYS - WROWS, 128), 1)
     key_feat[WROWS:] = jnp.where(lane == 3 * FEAT, 1.0, 0.0).astype(jnp.bfloat16)
+    fetch.wait()
+    fill_table(entries[...] * ROOT, table)
+    query_bias(0, spots, table, None, bias)
     for copy in copies:
         copy.wait()
 
 
 def prepare_second(
-    after, table, w_qkv, w_proj, w_up, w_down,
-    key_feat, bias, place, spread, v_qkv, v_proj, v_up, v_down, sems,
+    own, table, gain, offset, w_qkv, w_proj, w_up, w_down,
+    key_feat, bias, place, spread, query, kv, v_qkv, v_proj, v_up, v_down, sems,
 ):
-    del after
     copies = start_weights(
         1, (w_qkv, w_proj, w_up, w_down), (v_qkv, v_proj, v_up, v_down), sems
     )
@@ -275,8 +276,12 @@
     right = (c >= WLON).astype(jnp.int32)
     at = a * WLON + c - WLON * right
     spread[...] = onehot(jnp.where(right == side, at, PLANE + at), 2 * PLANE)
+    normed = layer_norm(own[...].astype(jnp.float32), gain[1, 0:1], offset[1, 0:1])
     for copy in copies:
         copy.wait()
+    packed = f32dot(normed.astype(jnp.bfloat16), v_qkv[...]).astype(jnp.bfloat16)
+    query[...] = packed[:, :D]
+    kv[...] = packed[:, D:]
 
 
 def first_kernel(
@@ -317,38 +322,34 @@
 
 
 def near_kernel(
-    own, lon, lat_a, lat_b, bias, key_feat,
-    gain, offset, w_qkv, w_proj, w_up, w_down, done, query_far, kv_far, kv,
+    own, query, kv_own, lon, lat_a, lat_b, bias, key_feat,
+    gain, offset, w_qkv, w_proj, w_up, w_down, done, kv_far, kv,
 ):
     gain, offset = gain.at[1], offset.at[1]
-    g0, o0 = gain[0:1], offset[0:1]
-    tokens = own[...].astype(jnp.float32)
-    normed = layer_norm(tokens, g0, o0).astype(jnp.bfloat16)
-    query = f32dot(normed, w_qkv[:, :D]).astype(jnp.bfloat16)
-    kv[:WROWS] = f32dot(normed, w_qkv[:, D:]).astype(jnp.bfloat16)
-    base = WROWS
+    base = 0
     for ref in (lon, lat_a, lat_b):
-        more = layer_norm(ref[...].astype(jnp.float32), g0, o0).astype(jnp.bfloat16)
-        kv[base : base + ref.shape[0]] = f32dot(more, w_qkv[:, D:]).astype(jnp.bfloat16)
+        more = layer_norm(ref[...].astype(jnp.float32), gain[0:1], offset[0:1])
+        kv[base : base + ref.shape[0]] = f32dot(more.astype(jnp.bfloat16), w_qkv[:, D:]).astype(
+            jnp.bfloat16
+        )
         base += ref.shape[0]
     parts = []
     for sa in range(2):
-        lat = WROWS + HALF + sa * 3 * QPAD
-        rows = (sa * QPAD, WROWS + sa * QPAD, lat, lat + 2 * QPAD)
-        window = jnp.concatenate([kv[r : r + QPAD] for r in rows], axis=0)
         q = slice(sa * QPAD, (sa + 1) * QPAD)
+        lat = HALF + sa * 3 * QPAD
+        window = jnp.concatenate(
+            [kv_own[q], kv[q], kv[lat : lat + QPAD], kv[lat + 2 * QPAD : lat + 3 * QPAD]], axis=0
+        )
         parts.append(attend(query[q], bias.at[q], window[:, :D], window[:, D:], key_feat[sa]))
-        kv_far[2 * sa * QPAD : (2 * sa + 1) * QPAD] = kv[HALF + sa * QPAD : HALF + (sa + 1) * QPAD]
-        kv_far[(2 * sa + 1) * QPAD : (2 * sa + 2) * QPAD] = kv[lat + QPAD : lat + 2 * QPAD]
-    query_far[...] = query[HALF:]
+        kv_far[sa * QPAD : (sa + 1) * QPAD] = kv[lat + QPAD : lat + 2 * QPAD]
     done[...] = finish(
-        tokens[:HALF], jnp.concatenate(parts, axis=0), gain[1:2], offset[1:2],
+        own[:HALF].astype(jnp.float32), jnp.concatenate(parts, axis=0), gain[1:2], offset[1:2],
         w_proj[...], w_up[...], w_down[...],
     )
 
 
 def far_kernel(
-    own, done, query, kv_near, lon, lat_a, lat_b, bias, key_feat, place,
+    own, done, query, kv_own, kv_lat, lon, lat_a, lat_b, bias, key_feat, place,
     gain, offset, w_qkv, w_proj, w_up, w_down, keep, send,
 ):
     gain, offset = gain.at[1], offset.at[1]
@@ -357,19 +358,12 @@
     kv = f32dot(normed, w_qkv[:, D:]).astype(jnp.bfloat16)
     parts = []
     for sa in range(2):
-        near = 2 * sa * QPAD
-        window = jnp.concatenate(
-            [
-                kv_near[near : near + QPAD],
-                kv[sa * QPAD : (sa + 1) * QPAD],
-                kv_near[near + QPAD : near + 2 * QPAD],
-                kv[(2 + sa) * QPAD : (3 + sa) * QPAD],
-            ],
-            axis=0,
-        )
         q = slice(sa * QPAD, (sa + 1) * QPAD)
         b = slice(HALF + sa * QPAD, HALF + (sa + 1) * QPAD)
-        parts.append(attend(query[q], bias.at[b], window[:, :D], window[:, D:], key_feat[2 + sa]))
+        window = jnp.concatenate(
+            [kv_own[b], kv[q], kv_lat[q], kv[(2 + sa) * QPAD : (3 + sa) * QPAD]], axis=0
+        )
+        parts.append(attend(query[b], bias.at[b], window[:, :D], window[:, D:], key_feat[2 + sa]))
     result = finish(
         own[HALF:].astype(jnp.float32), jnp.concatenate(parts, axis=0), gain[1:2], offset[1:2],
         w_proj[...], w_up[...], w_down[...],
@@ -434,18 +428,19 @@
         pltpu.with_memory_space_constraint(w, pltpu.HBM) for w in (w_qkv, w_proj, w_up, w_down)
     )
     shapes = [w.shape[1:] for w in raw]
-    sems = [pltpu.SemaphoreType.DMA((len(raw),))]
+    sems = [pltpu.SemaphoreType.DMA((len(raw) + 1,))]
 
     plane = tokens.reshape(2 * PLANE, D)
     (cut,) = call(cut_kernel, [(PLANE, D)], (plane,), flops=10**7)
     other = swap(cut, "lev")
+    entries = rel_bias.reshape(2 * HEADS, rel_bias.shape[-1])
     pick, feat_first, bias_first, table, *weights = call(
         prepare_first,
         [(WROWS, 3 * PLANE), (KEYS, 128), (WROWS, HEADS * 128), (FROWS * 2 * HEADS, 128)] + shapes,
-        (rel_bias.reshape(2 * HEADS, rel_bias.shape[-1]),) + raw,
-        scratch=sems,
+        (pltpu.with_memory_space_constraint(entries, pltpu.HBM),) + raw,
+        scratch=[pltpu.VMEM(entries.shape, jnp.float32)] + sems,
         flops=10**8,
-        skip=(1, 2, 3, 4),
+        skip=(0, 1, 2, 3, 4),
         wide=(3,),
     )
     first, near, far = call(
@@ -455,25 +450,27 @@
         flops=2 * 10**9,
     )
 
+    lon_a = swap(near, "lev")
     lon_b = swap(far, "lon")
-    lon_a = swap(near, "lev")
-    feat_second, bias_second, place, spread, *weights = call(
+    feat_second, bias_second, place, spread, query, kv_own, *weights = call(
         prepare_second,
-        [(4, KEYS, 128), (WROWS, HEADS * 128), (2 * PLANE, WROWS), (2 * PLANE, 2 * PLANE)] + shapes,
-        (first, table) + raw,
+        [(4, KEYS, 128), (WROWS, HEADS * 128), (2 * PLANE, WROWS), (2 * PLANE, 2 * PLANE)]
+        + [(WROWS, D), (WROWS, 2 * D)]
+        + shapes,
+        (first, table) + norms + raw,
         scratch=sems,
-        flops=10**8,
-        skip=(2, 3, 4, 5),
+        flops=10**9,
+        skip=(4, 5, 6, 7),
     )
     weights = norms + tuple(weights)
     strip_a, strip_b = call(strip_kernel, [(3 * QPAD, D)] * 2, (first, lon_a), flops=10**6)
     lat_b = swap(strip_b, "lat_b")
     lat_a = swap(strip_a, "lat_a")
-    done, query_far, kv_far = call(
+    done, kv_lat = call(
         near_kernel,
-        [(HALF, D), (HALF, D), (WROWS, 2 * D)],
-        (first, lon_a, lat_a, lat_b, bias_second, feat_second) + weights,
-        scratch=[pltpu.VMEM((WROWS + HALF + 6 * QPAD, 2 * D), jnp.bfloat16)],
+        [(HALF, D), (HALF, 2 * D)],
+        (first, query, kv_own, lon_a, lat_a, lat_b, bias_second, feat_second) + weights,
+        scratch=[pltpu.VMEM((HALF + 6 * QPAD, 2 * D), jnp.bfloat16)],
         flops=2 * 10**9,
     )
 
@@ -483,7 +480,8 @@
     keep, send = call(
         far_kernel,
         [(PLANE, D), (PLANE, D)],
-        (first, done, query_far, kv_far, lon_b, corner_a, corner_b, bias_second, feat_second, place)
+        (first, done, query, kv_own, kv_lat, lon_b, corner_a, corner_b)
+        + (bias_second, feat_second, place)
         + weights,
         flops=2 * 10**9,
     )

time: 72.2 us -> 71.6 us (level)
    unnamed x10 -> x8, local copies, waits for them, and re-layouts: 1.63 us -> 0.93 us
  transfers between devices with their start and end apart: 8 -> 8, of which waited for: 3 -> 3; matrix products, arithmetic and copies ran while one was open for 0% -> 0% of each run, Pallas kernels for 12% -> 13%
where the time goes in v1:
time: 71.6 us; the launch traced here: 71.3 us
  starting transfers between devices  44.6 us (62%)
  Pallas kernels  17.1 us (24%)
  waiting for transfers between devices  8.51 us (12%)
  local copies, waits for them, and re-layouts  0.93 us (1%)
    ppermute x8, starting transfers between devices, shards(): swap = lambda x, name: lax.ppermute(x, AXES, send_to[name])  44.6 us
    pallas_call x9, Pallas kernels, call(): pl.pallas_call(kernel, out_shape=[jax.ShapeDtypeStruct(s, jnp.float32 if...  17.1 us
    ppermute x8, waiting for transfers between devices, shards(): swap = lambda x, name: lax.ppermute(x, AXES, send_to[name])  8.51 us
  transfers between devices with their start and end apart: 8, of which 3 were waited for; matrix products, arithmetic and copies ran while one was open for 0% of the time, Pallas kernels for 13%

profile of v1, /device:TPU:4, one launch (start us, length us, event | category | flops | bytes accessed | tf_op | source)
XLA Modules:
  0.0 71.3 jit_solution(17494419747522743979)
XLA Ops:
  0.0 0.0 copy-start
  0.0 0.9 %copy-done = bf16[1,6,24,512]{3,2,1,0:T(8,128)(2,1)S(1)} copy-done((bf16[1,6,24,512]{3,2,1,0:T(8,128)(2,1)S(1)}, bf16[1,6,24,512]{3,2,1,0:T(8,128)(2,1)}, u32[]{:S(2)}) %copy-start) | copy-done | bytes 147480
  0.9 0.2 shard_map.82
  1.1 3.1 %collective-permute-start = (bf16[72,512]{1,0:T(8,128)(2,1)S(1)}, bf16[72,512]{1,0:T(8,128)(2,1)S(1)}, u32[]{:S(2)}, u32[]{:S(2)}) collective-permute-start(bf16[72,512]{1,0:T(8,128)(2,1)S(1)} %shard_map.82), channel_id=1, source_target_pairs={{0,1},{1,0},{2,3},{3,2},{4,5},{5,4},{6,7},{7,6},{8,9},{9,8},{10,11... | collective-permute-start | bytes 221192 | tf_op jit(solution)/shard_map/ppermute | solution.py:425
  4.2 0.0 copy-start.1
  4.2 0.0 copy-start.2
  4.2 0.0 copy-start.3
  4.2 2.3 %shard_map.83 = (bf16[192,216]{1,0:T(8,128)(2,1)S(1)}, bf16[256,128]{1,0:T(8,128)(2,1)S(1)}, bf16[192,2048]{1,0:T(8,128)(2,1)S(1)}, f32[768,128]{1,0:T(8,128)S(1...) custom-call(f32[32,37]{1,0:T(8,128)} %bitcast.5, ...), custom_call_target="tpu_custom_call" | custom-call | flops 100000000 | bytes 1048576 | tf_op jit(solution)/shard_map/pallas_call | solution.py:385
  6.5 0.8 %collective-permute-done.other = bf16[72,512]{1,0:T(8,128)(2,1)S(1)} collective-permute-done((bf16[72,512]{1,0:T(8,128)(2,1)S(1)}, bf16[72,512]{1,0:T(8,128)(2,1)S(1)}, u32[]{:S(2)}, u32[]{:S(2)}) %collective-permute-start) | collective-permute-done | bytes 73760 | tf_op jit(solution)/shard_map/ppermute | solution.py:425
  7.3 0.0 copy-done.1
  7.3 0.0 copy-done.2
  7.3 0.0 copy-done.3
  7.3 3.2 %shard_map.84 = (bf16[192,512]{1,0:T(8,128)(2,1)S(1)}, bf16[96,512]{1,0:T(8,128)(2,1)S(1)}, bf16[96,512]{1,0:T(8,128)(2,1)S(1)}) custom-call(bf16[144,512]{1,0:T(8,128)(2,1)S(1)} %bitcast.4, bf16[72,512]{1,0:T(8,128)(2,1)S(1)} %collective-permute-done.other, bf16[192,216]{1,0:T(8,128)(2,1)S(1)} %get-tuple-element.34.pick, ...), custom_call_target="tpu_custom_call" | custom-call | flops 2000000000 | bytes 1048576 | tf_op jit(solution)/shard_map/pallas_call | solution.py:385
  10.5 3.1 %collective-permute-start.1 = (bf16[96,512]{1,0:T(8,128)(2,1)S(1)}, bf16[96,512]{1,0:T(8,128)(2,1)S(1)}, u32[]{:S(2)}, u32[]{:S(2)}) collective-permute-start(bf16[96,512]{1,0:T(8,128)(2,1)S(1)} %get-tuple-element.45), channel_id=1, source_target_pairs={{0,1},{1,0},{2,3},{3,2},{4,5},{5,4},{6,7},{7,6},{8,9},{9,8},{10,11... | collective-permute-start | bytes 294920 | tf_op jit(solution)/shard_map/ppermute | solution.py:425
  13.6 3.4 %collective-permute-done.1.lon = bf16[96,512]{1,0:T(8,128)(2,1)S(1)} collective-permute-done((bf16[96,512]{1,0:T(8,128)(2,1)S(1)}, bf16[96,512]{1,0:T(8,128)(2,1)S(1)}, u32[]{:S(2)}, u32[]{:S(2)}) %collective-permute-start.1) | collective-permute-done | bytes 98336 | tf_op jit(solution)/shard_map/ppermute | solution.py:425
  17.0 1.9 %collective-permute-start.2 = (bf16[144,512]{1,0:T(8,128)(2,1)S(1)}, bf16[144,512]{1,0:T(8,128)(2,1)S(1)}, u32[]{:S(2)}, u32[]{:S(2)}) collective-permute-start(bf16[144,512]{1,0:T(8,128)(2,1)S(1)} %get-tuple-element.46), channel_id=1, source_target_pairs={{0,64},{1,65},{2,66},{3,67},{4,68},{5,69},{6,70},{7,71},{8,72},{9,... | collective-permute-start | bytes 442376 | tf_op jit(solution)/shard_map/ppermute | solution.py:425
  19.0 12.8 %collective-permute-start.3 = (bf16[144,512]{1,0:T(8,128)(2,1)S(1)}, bf16[144,512]{1,0:T(8,128)(2,1)S(1)}, u32[]{:S(2)}, u32[]{:S(2)}) collective-permute-start(bf16[144,512]{1,0:T(8,128)(2,1)S(1)} %get-tuple-element.47), channel_id=1, source_target_pairs={{0,704},{1,705},{2,706},{3,707},{4,708},{5,709},{6,710},{7,711},{8... | collective-permute-start | bytes 442376 | tf_op jit(solution)/shard_map/ppermute | solution.py:425
  31.8 12.9 %collective-permute-start.4 = (bf16[96,512]{1,0:T(8,128)(2,1)S(1)}, bf16[96,512]{1,0:T(8,128)(2,1)S(1)}, u32[]{:S(2)}, u32[]{:S(2)}) collective-permute-start(bf16[96,512]{1,0:T(8,128)(2,1)S(1)} %get-tuple-element.56), channel_id=1, source_target_pairs={{0,60},{1,5},{2,62},{3,7},{4,8},{5,1},{6,10},{7,3},{8,4},{9,13},{1... | collective-permute-start | bytes 294920 | tf_op jit(solution)/shard_map/ppermute | solution.py:425
  44.8 3.2 %shard_map.85 = (bf16[4,256,128]{2,1,0:T(8,128)(2,1)S(1)}, bf16[192,2048]{1,0:T(8,128)(2,1)S(1)}, bf16[144,192]{1,0:T(8,128)(2,1)S(1)}, bf16[144,144]{1,0:T(8,12...) custom-call(bf16[192,512]{1,0:T(8,128)(2,1)S(1)} %get-tuple-element., ...), custom_call_target="tpu_custom_call" | custom-call | flops 1000000000 | bytes 1048576 | tf_op jit(solution)/shard_map/pallas_call | solution.py:385
  47.9 0.0 collective-permute-done.4.lon
  48.0 1.9 %collective-permute-start.5 = (bf16[48,512]{1,0:T(8,128)(2,1)S(1)}, bf16[48,512]{1,0:T(8,128)(2,1)S(1)}, u32[]{:S(2)}, u32[]{:S(2)}) collective-permute-start(bf16[48,512]{1,0:T(8,128)(2,1)S(1)} %get-tuple-element.57), channel_id=1, source_target_pairs={{0,64},{1,65},{2,66},{3,67},{4,68},{5,69},{6,70},{7,71},{8,72},{9,... | collective-permute-start | bytes 147464 | tf_op jit(solution)/shard_map/ppermute | solution.py:425
  49.9 6.9 %collective-permute-start.6 = (bf16[48,512]{1,0:T(8,128)(2,1)S(1)}, bf16[48,512]{1,0:T(8,128)(2,1)S(1)}, u32[]{:S(2)}, u32[]{:S(2)}) collective-permute-start(bf16[48,512]{1,0:T(8,128)(2,1)S(1)} %get-tuple-element.58), channel_id=1, source_target_pairs={{0,764},{1,709},{2,766},{3,711},{4,712},{5,705},{6,714},{7,707},{8... | collective-permute-start | bytes 147464 | tf_op jit(solution)/shard_map/ppermute | solution.py:425
  56.8 0.0 collective-permute-done.2.lat_a
  56.8 0.0 collective-permute-done.3.lat_b
  56.8 3.6 %shard_map.87 = (bf16[96,512]{1,0:T(8,128)(2,1)S(1)}, bf16[96,1024]{1,0:T(8,128)(2,1)S(1)}) custom-call(bf16[192,512]{1,0:T(8,128)(2,1)S(1)} %get-tuple-element.41.own, bf16[192,512]{1,0:T(8,128)(2,1)S(1)} %get-tuple-element.43.query, bf16[192,1024]{1,0:T(8,128)(2,1)S(1)} %get-tuple-element.44.kv_own, bf16[96,512]{1,0:T(8,128)(2,1)S(1)} %collective-permute-done.1.lon, ...), custom_call_target="tpu_custom_call" | custom-call | flops 2000000000 | bytes 1048576 | tf_op jit(solution)/shard_map/pallas_call | solution.py:385
  60.4 0.0 collective-permute-done.5.lat_a
  60.4 0.0 collective-permute-done.6.lat_b
  60.4 3.7 %shard_map.89 = (bf16[72,512]{1,0:T(8,128)(2,1)S(1)}, bf16[72,512]{1,0:T(8,128)(2,1)S(1)}) custom-call(bf16[192,512]{1,0:T(8,128)(2,1)S(1)} %get-tuple-element.41.own, bf16[96,512]{1,0:T(8,128)(2,1)S(1)} %get-tuple-element.54.done, bf16[192,512]{1,0:T(8,128)(2,1)S(1)} %get-tuple-element.43.query, bf16[192,1024]{1,0:T(8,128)(2,1)S(1)} %get-tuple-element.44.kv_own, ...), custom_call_target="tpu_custom_call" | custom-call | flops 2000000000 | bytes 1048576 | tf_op jit(solution)/shard_map/pallas_call | solution.py:385
  64.1 1.9 %collective-permute-start.7 = (bf16[72,512]{1,0:T(8,128)(2,1)S(1)}, bf16[72,512]{1,0:T(8,128)(2,1)S(1)}, u32[]{:S(2)}, u32[]{:S(2)}) collective-permute-start(bf16[72,512]{1,0:T(8,128)(2,1)S(1)} %get-tuple-element.61), channel_id=1, source_target_pairs={{0,1},{1,0},{2,3},{3,2},{4,5},{5,4},{6,7},{7,6},{8,9},{9,8},{10,11... | collective-permute-start | bytes 221192 | tf_op jit(solution)/shard_map/ppermute | solution.py:425
  66.0 4.3 %collective-permute-done.7.theirs = bf16[72,512]{1,0:T(8,128)(2,1)S(1)} collective-permute-done((bf16[72,512]{1,0:T(8,128)(2,1)S(1)}, bf16[72,512]{1,0:T(8,128)(2,1)S(1)}, u32[]{:S(2)}, u32[]{:S(2)}) %collective-permute-start.7) | collective-permute-done | bytes 73760 | tf_op jit(solution)/shard_map/ppermute | solution.py:425
  70.4 0.9 %shard_map.90 = bf16[144,512]{1,0:T(8,128)(2,1)} custom-call(bf16[72,512]{1,0:T(8,128)(2,1)S(1)} %get-tuple-element.60.mine, bf16[72,512]{1,0:T(8,128)(2,1)S(1)} %collective-permute-done.7.theirs, bf16[144,144]{1,0:T(8,128)(2,1)S(1)} %get-tuple-element.62.spread), custom_call_target="tpu_custom_call" | custom-call | flops 100000000 | bytes 1048576 | tf_op jit(solution)/shard_map/pallas_call | solution.py:385
  (2 shorter events, 0.0 us)
Async XLA Ops:
  0.0 0.9 %copy-start = (bf16[1,6,24,512]{3,2,1,0:T(8,128)(2,1)S(1)}, bf16[1,6,24,512]{3,2,1,0:T(8,128)(2,1)}, u32[]{:S(2)}) copy-start(bf16[1,6,24,512]{3,2,1,0:T(8,128)(2,1)} %param.8) | copy-start | bytes 442372
  1.1 6.2 %collective-permute-start = (bf16[72,512]{1,0:T(8,128)(2,1)S(1)}, bf16[72,512]{1,0:T(8,128)(2,1)S(1)}, u32[]{:S(2)}, u32[]{:S(2)}) collective-permute-start(bf16[72,512]{1,0:T(8,128)(2,1)S(1)} %shard_map.82), channel_id=1, source_target_pairs={{0,1},{1,0},{2,3},{3,2},{4,5},{5,4},{6,7},{7,6},{8,9},{9,8},{10,11... | collective-permute-start | bytes 221192 | tf_op jit(solution)/shard_map/ppermute | solution.py:425
  4.2 3.1 %copy-start.1 = (bf16[1,6,24,512]{3,2,1,0:T(8,128)(2,1)S(1)}, bf16[1,6,24,512]{3,2,1,0:T(8,128)(2,1)}, u32[]{:S(2)}) copy-start(bf16[1,6,24,512]{3,2,1,0:T(8,128)(2,1)} %param.8) | copy-start | bytes 442372
  4.2 3.1 %copy-start.2 = (f32[2,2,512]{2,1,0:T(2,128)S(1)}, f32[2,2,512]{2,1,0:T(2,128)}, u32[]{:S(2)}) copy-start(f32[2,2,512]{2,1,0:T(2,128)} %gain.7) | copy-start | bytes 24580
  4.2 3.1 %copy-start.3 = (f32[2,2,512]{2,1,0:T(2,128)S(1)}, f32[2,2,512]{2,1,0:T(2,128)}, u32[]{:S(2)}) copy-start(f32[2,2,512]{2,1,0:T(2,128)} %offset.7) | copy-start | bytes 24580
  10.5 6.5 %collective-permute-start.1 = (bf16[96,512]{1,0:T(8,128)(2,1)S(1)}, bf16[96,512]{1,0:T(8,128)(2,1)S(1)}, u32[]{:S(2)}, u32[]{:S(2)}) collective-permute-start(bf16[96,512]{1,0:T(8,128)(2,1)S(1)} %get-tuple-element.45), channel_id=1, source_target_pairs={{0,1},{1,0},{2,3},{3,2},{4,5},{5,4},{6,7},{7,6},{8,9},{9,8},{10,11... | collective-permute-start | bytes 294920 | tf_op jit(solution)/shard_map/ppermute | solution.py:425
  17.0 39.7 %collective-permute-start.2 = (bf16[144,512]{1,0:T(8,128)(2,1)S(1)}, bf16[144,512]{1,0:T(8,128)(2,1)S(1)}, u32[]{:S(2)}, u32[]{:S(2)}) collective-permute-start(bf16[144,512]{1,0:T(8,128)(2,1)S(1)} %get-tuple-element.46), channel_id=1, source_target_pairs={{0,64},{1,65},{2,66},{3,67},{4,68},{5,69},{6,70},{7,71},{8,72},{9,... | collective-permute-start | bytes 442376 | tf_op jit(solution)/shard_map/ppermute | solution.py:425
  19.0 37.8 %collective-permute-start.3 = (bf16[144,512]{1,0:T(8,128)(2,1)S(1)}, bf16[144,512]{1,0:T(8,128)(2,1)S(1)}, u32[]{:S(2)}, u32[]{:S(2)}) collective-permute-start(bf16[144,512]{1,0:T(8,128)(2,1)S(1)} %get-tuple-element.47), channel_id=1, source_target_pairs={{0,704},{1,705},{2,706},{3,707},{4,708},{5,709},{6,710},{7,711},{8... | collective-permute-start | bytes 442376 | tf_op jit(solution)/shard_map/ppermute | solution.py:425
  31.8 16.1 %collective-permute-start.4 = (bf16[96,512]{1,0:T(8,128)(2,1)S(1)}, bf16[96,512]{1,0:T(8,128)(2,1)S(1)}, u32[]{:S(2)}, u32[]{:S(2)}) collective-permute-start(bf16[96,512]{1,0:T(8,128)(2,1)S(1)} %get-tuple-element.56), channel_id=1, source_target_pairs={{0,60},{1,5},{2,62},{3,7},{4,8},{5,1},{6,10},{7,3},{8,4},{9,13},{1... | collective-permute-start | bytes 294920 | tf_op jit(solution)/shard_map/ppermute | solution.py:425
  48.0 12.4 %collective-permute-start.5 = (bf16[48,512]{1,0:T(8,128)(2,1)S(1)}, bf16[48,512]{1,0:T(8,128)(2,1)S(1)}, u32[]{:S(2)}, u32[]{:S(2)}) collective-permute-start(bf16[48,512]{1,0:T(8,128)(2,1)S(1)} %get-tuple-element.57), channel_id=1, source_target_pairs={{0,64},{1,65},{2,66},{3,67},{4,68},{5,69},{6,70},{7,71},{8,72},{9,... | collective-permute-start | bytes 147464 | tf_op jit(solution)/shard_map/ppermute | solution.py:425
  49.9 10.5 %collective-permute-start.6 = (bf16[48,512]{1,0:T(8,128)(2,1)S(1)}, bf16[48,512]{1,0:T(8,128)(2,1)S(1)}, u32[]{:S(2)}, u32[]{:S(2)}) collective-permute-start(bf16[48,512]{1,0:T(8,128)(2,1)S(1)} %get-tuple-element.58), channel_id=1, source_target_pairs={{0,764},{1,709},{2,766},{3,711},{4,712},{5,705},{6,714},{7,707},{8... | collective-permute-start | bytes 147464 | tf_op jit(solution)/shard_map/ppermute | solution.py:425
  64.1 6.2 %collective-permute-start.7 = (bf16[72,512]{1,0:T(8,128)(2,1)S(1)}, bf16[72,512]{1,0:T(8,128)(2,1)S(1)}, u32[]{:S(2)}, u32[]{:S(2)}) collective-permute-start(bf16[72,512]{1,0:T(8,128)(2,1)S(1)} %get-tuple-element.61), channel_id=1, source_target_pairs={{0,1},{1,0},{2,3},{3,2},{4,5},{5,4},{6,7},{7,6},{8,9},{9,8},{10,11... | collective-permute-start | bytes 221192 | tf_op jit(solution)/shard_map/ppermute | solution.py:425
